TPU v7x, 32 devices: a whole 2x2x4 slice. The times are simulated.
32 devices in a mesh: sub: 8 (over y, x, core), coarse: 4 (over z).
Axes of the slice: x: 2, y: 2, z: 4, core: 2. Of those that a mesh axis runs over, the one named last changes fastest.
Arguments:
- right_side: float32 [8, 4, 128, 128], P('sub', 'coarse'), may hold values from -150 to 150
- diagonal: float32 [8, 4, 128, 128], P('sub', 'coarse'), may hold values from 2 to 8
- cell_link: float32 [8, 4, 128, 128], P('sub', 'coarse'), may hold values from 0.2 to 0.9
- block_inverse: float32 [8, 4, 128, 128, 128], P('sub', 'coarse'), may hold values from -1 to 1
- coupling: float32 [8, 4, 4, 128, 128], P('sub', 'coarse'), may hold values from -0.26516503 to 0.26516503
- coarse_basis: float32 [8, 4, 128, 128], P('sub', 'coarse'), may hold values from -6 to 6
- coarse_inverse: float32 [512, 512], P('coarse'), may hold values from -0.25 to 0.25
- partner: int32 [8, 4], P('sub'), may hold values from 0 to 7, as said below
- margin_width: int32 [8, 4], P('sub'), may hold values from 4 to 8, as said below
- margin_blocks: int32 [8, 4, 4, 8], P('sub', 'coarse'), may hold values from 0 to 127
- aggregate: int32 [8, 4, 128], P('sub', 'coarse'), may hold values from 0 to 511, as said below
Outputs:
- solution: float32 [8, 4, 128, 128], P('sub', 'coarse')
Inputs may be any that keep to these rules, and one draw needn't show every extreme that they name: partner[s, r] differs from s, partner[partner[s, r], r] = s, and the 4 partners of one subdomain are distinct. margin_width[partner[s, r], r] = margin_width[s, r]; every colour round has a pair with width 8. `margin_blocks`: entries with w >= margin_width[s, r] are not used. aggregate[s, c, b] lies in (s * 4 + c) * 16 to (s * 4 + c + 1) * 16 - 1, and every one of these 16 aggregates has a block of part [s, c].
All inputs are finite; a program needn't handle non-finite values.
Results may differ from a plain program's by a relative error of at most 0.0003.
Values sent between devices are 32-bit elements; how exact they have to be, the bound alone decides.
No kernel may reach another device: no remote copies, remote signals or barrier semaphores. Data moves between devices by JAX's collectives and lax.ppermute only.
A program may use at most 64 MiB of HBM per device.

v0:
```python
import jax
import jax.numpy as jnp
from jax import lax
from jax.sharding import PartitionSpec as P

BS = 128
BPD = 128
AGG_DEV = 16
ITERS = 4


def givens_solve(columns, beta):
    steps_count = len(columns)
    cosines = []
    sines = []
    side_terms = [beta] + [jnp.zeros_like(beta) for unused in range(steps_count)]
    triangle = []
    for column_id in range(steps_count):
        column = list(columns[column_id])
        for row_id in range(column_id):
            upper = column[row_id]
            lower = column[row_id + 1]
            column[row_id] = cosines[row_id] * upper + sines[row_id] * lower
            column[row_id + 1] = cosines[row_id] * lower - sines[row_id] * upper
        upper = column[column_id]
        lower = column[column_id + 1]
        radius = jnp.sqrt(upper * upper + lower * lower)
        cosine = upper / radius
        sine_value = lower / radius
        column[column_id] = radius
        cosines.append(cosine)
        sines.append(sine_value)
        side_terms[column_id + 1] = -sine_value * side_terms[column_id]
        side_terms[column_id] = cosine * side_terms[column_id]
        triangle.append(column)
    weights = [None] * steps_count
    for column_id in reversed(range(steps_count)):
        running = side_terms[column_id]
        for later_col in range(column_id + 1, steps_count):
            running = running - triangle[later_col][column_id] * weights[later_col]
        weights[column_id] = running / triangle[column_id][column_id]
    return weights


def on_device(
    right_side,
    diagonal,
    cell_link,
    block_inverse,
    coupling,
    coarse_basis,
    coarse_inverse,
    partner,
    margin_width,
    margin_blocks,
    aggregate,
):
    highest = lax.Precision.HIGHEST
    block_count = right_side.shape[2]
    unknowns = right_side.shape[3]
    factor = (BS * BPD / AGG_DEV) ** (-0.5)
    inverse_blocks = block_inverse[0, 0]
    couplings = coupling[0, 0]
    basis_local = coarse_basis[0, 0]
    diagonal_local = diagonal[0, 0]
    link_local = cell_link[0, 0]
    paired = partner[0]
    widths = margin_width[0]
    blocks = margin_blocks[0, 0]
    member_of = aggregate[0, 0]
    aggregate_count = coarse_inverse.shape[1]
    member_table = (member_of[:, None] == jnp.arange(aggregate_count)[None, :]).astype(jnp.float32)
    rounds = blocks.shape[0]
    widest = blocks.shape[1]
    target = (blocks.reshape(-1)[:, None] == jnp.arange(block_count)[None, :]).astype(jnp.float32)
    live_mask = (jnp.arange(widest)[None, :] < widths[:, None]).astype(jnp.float32)

    def margin(values):
        outgoing = jnp.take(values, blocks.reshape(-1), axis=0).reshape(rounds, widest, unknowns)
        pieces = []
        for round_id in range(rounds):
            gathered = lax.all_gather(outgoing[round_id], "sub", axis=0, tiled=True)
            pieces.append(lax.dynamic_slice_in_dim(gathered, paired[round_id] * widest, widest, 0))
        incoming = jnp.stack(pieces)
        mapped = (
            jnp.einsum("rij,rwj->rwi", couplings, incoming, precision=highest)
            * live_mask[:, :, None]
        )
        return jnp.einsum(
            "kb,ki->bi", target, mapped.reshape(rounds * widest, unknowns), precision=highest
        )

    def squared_norm(values):
        return lax.psum(jnp.sum(values * values), ("sub", "coarse"))

    start_vector = right_side[0, 0]
    directions = []
    columns = []
    beta = jnp.sqrt(squared_norm(start_vector))
    basis_list = [start_vector / beta]
    for krylov_step in range(ITERS):
        current = basis_list[-1]
        inner = jnp.sum(basis_local * current, axis=1)
        restricted = lax.psum(
            jnp.dot(inner, member_table, precision=highest) * factor, ("sub", "coarse")
        )
        local_part = jnp.einsum(
            "bij,bj->bi", inverse_blocks, current + margin(current), precision=highest
        )
        coarse_part = jnp.dot(coarse_inverse, restricted, precision=highest)
        coarse_full = lax.all_gather(coarse_part, "coarse", axis=0, tiled=True)
        prolonged = jnp.dot(member_table, coarse_full, precision=highest)
        direction = local_part + prolonged[:, None] * basis_local
        directions.append(direction)
        flat_line = direction.reshape(-1)
        link_line = link_local.reshape(-1)
        zero_pad = jnp.zeros((1,), jnp.float32)
        ahead_terms = jnp.concatenate([flat_line[1:], zero_pad]) * link_line
        behind_terms = jnp.concatenate([zero_pad, (link_line * flat_line)[:-1]])
        product = (
            diagonal_local * direction
            - (ahead_terms + behind_terms).reshape(direction.shape)
            - margin(direction)
        )
        projected = lax.psum(
            jnp.stack([jnp.sum(vector * product) for vector in basis_list]), ("sub", "coarse")
        )
        for position in range(len(basis_list)):
            product = product - projected[position] * basis_list[position]
        norm_new = jnp.sqrt(squared_norm(product))
        columns.append([projected[position] for position in range(len(basis_list))] + [norm_new])
        basis_list.append(product / norm_new)
    weights = givens_solve(columns, beta)
    solution = weights[0] * directions[0]
    for position in range(1, ITERS):
        solution = solution + weights[position] * directions[position]
    return solution.reshape(right_side.shape)


def solution(mesh):
    placed = (
        P("sub", "coarse", None, None),
        P("sub", "coarse", None, None),
        P("sub", "coarse", None, None),
        P("sub", "coarse", None, None, None),
        P("sub", "coarse", None, None, None),
        P("sub", "coarse", None, None),
        P("coarse", None),
        P("sub", None),
        P("sub", None),
        P("sub", "coarse", None, None),
        P("sub", "coarse", None),
    )
    return jax.shard_map(
        on_device,
        mesh=mesh,
        in_specs=placed,
        out_specs=P("sub", "coarse", None, None),
        check_vma=False,
    )
```

profile of v0, /device:TPU:0, one launch (start us, length us, event | category | flops | bytes accessed | tf_op | source)
XLA Modules:
  0.0 958.9 jit_solution(15861982066872133460)
XLA Ops:
  2.3 42.2 %psum.91 = f32[]{:T(128)} all-reduce(f32[]{:T(128)} %multiply_reduce_fusion.14), channel_id=1, replica_groups=mesh['sub'=8,'coarse'=4] {'sub','coarse'}, use_global_device_ids=true, to_apply=%region_1.0 | all-reduce | flops 1 | bytes 8 | tf_op jit(solution)/shard_map/psum | solution.py:94
  46.9 10.0 %all_gather.108 = f32[64,128]{1,0:T(8,128)S(1)} all-gather(f32[8,128]{1,0:T(8,128)S(1)} %get-tuple-element.63), channel_id=1, replica_groups=mesh['sub'=8,'coarse'=4] {'sub'}, dimensions={0}, use_global_device_ids=true | all-gather | bytes 36864 | tf_op jit(solution)/shard_map/all_gather | solution.py:82
  59.0 8.1 all_gather.109
  67.9 9.1 all_gather.110
  77.6 8.1 all_gather.111
  87.8 15.4 %fusion.6 = f32[128,1,128]{2,1,0:T(1,128)S(1)} fusion(f32[128,128,1]{1,2,0:T(1,128)S(1)} %bitcast.355, f32[1,1,128,128,128]{4,3,2,1,0:T(8,128)} %param.16), kind=kOutput, calls=%fused_computation.14 | convolution fusion | flops 25165824 | bytes 8519680 | tf_op jit(solution)/shard_map/bij,bj->bi/dot_general | solution.py:107
  103.5 39.4 %psum.92 = f32[512]{0:T(512)S(1)} all-reduce(f32[512]{0:T(512)S(1)} %broadcast_multiply_fusion.3), channel_id=1, replica_groups=mesh['sub'=8,'coarse'=4] {'sub','coarse'}, use_global_device_ids=true, to_apply=%region_3.5 | all-reduce | flops 512 | bytes 4096 | tf_op jit(solution)/shard_map/psum | solution.py:104
  143.1 9.8 %all-gather = f32[4,1,128]{2,1,0:T(1,128)S(1)} all-gather(f32[1,1,128]{2,1,0:T(1,128)S(1)} %convolution_bitcast_fusion.7), channel_id=1, replica_groups=mesh['sub'=8,'coarse'=4] {'coarse'}, dimensions={0}, use_global_device_ids=true | all-gather | bytes 2560 | tf_op jit(solution)/shard_map/all_gather | solution.py:111
  153.9 9.8 %all_gather.113 = f32[64,128]{1,0:T(8,128)S(1)} all-gather(f32[8,128]{1,0:T(8,128)S(1)} %get-tuple-element.59), channel_id=1, replica_groups=mesh['sub'=8,'coarse'=4] {'sub'}, dimensions={0}, use_global_device_ids=true | all-gather | bytes 36864 | tf_op jit(solution)/shard_map/all_gather | solution.py:82
  163.8 9.1 all_gather.114
  180.9 9.1 all_gather.116
  191.5 37.8 %psum.93 = f32[]{:T(128)} all-reduce(f32[]{:T(128)} %get-tuple-element.80), channel_id=1, replica_groups=mesh['sub'=8,'coarse'=4] {'sub','coarse'}, use_global_device_ids=true, to_apply=%region_5.7 | all-reduce | flops 1 | bytes 8 | tf_op jit(solution)/shard_map/psum | solution.py:125
  230.6 41.2 %psum.94 = f32[]{:T(128)} all-reduce(f32[]{:T(128)} %multiply_reduce_fusion.12), channel_id=1, replica_groups=mesh['sub'=8,'coarse'=4] {'sub','coarse'}, use_global_device_ids=true, to_apply=%region_7.9 | all-reduce | flops 1 | bytes 8 | tf_op jit(solution)/shard_map/psum | solution.py:94
  274.0 10.1 %all_gather.117 = f32[64,128]{1,0:T(8,128)S(1)} all-gather(f32[8,128]{1,0:T(8,128)S(1)} %get-tuple-element.55), channel_id=1, replica_groups=mesh['sub'=8,'coarse'=4] {'sub'}, dimensions={0}, use_global_device_ids=true | all-gather | bytes 36864 | tf_op jit(solution)/shard_map/all_gather | solution.py:82
  284.1 9.0 all_gather.118
  301.2 9.0 all_gather.120
  311.1 15.4 %fusion.4 = f32[128,1,128]{2,1,0:T(1,128)S(1)} fusion(f32[128,128,1]{1,2,0:T(1,128)S(1)} %bitcast.356, f32[1,1,128,128,128]{4,3,2,1,0:T(8,128)} %param.16), kind=kOutput, calls=%fused_computation.12 | convolution fusion | flops 25165824 | bytes 8519680 | tf_op jit(solution)/shard_map/bij,bj->bi/dot_general | solution.py:107
  326.8 37.7 %psum.95 = f32[512]{0:T(512)S(1)} all-reduce(f32[512]{0:T(512)S(1)} %broadcast_multiply_fusion.2), channel_id=1, replica_groups=mesh['sub'=8,'coarse'=4] {'sub','coarse'}, use_global_device_ids=true, to_apply=%region_9.11 | all-reduce | flops 512 | bytes 4096 | tf_op jit(solution)/shard_map/psum | solution.py:104
  364.7 9.6 %all-gather.1 = f32[4,1,128]{2,1,0:T(1,128)S(1)} all-gather(f32[1,1,128]{2,1,0:T(1,128)S(1)} %convolution_bitcast_fusion.5), channel_id=1, replica_groups=mesh['sub'=8,'coarse'=4] {'coarse'}, dimensions={0}, use_global_device_ids=true | all-gather | bytes 2560 | tf_op jit(solution)/shard_map/all_gather | solution.py:111
  375.4 9.8 %all_gather.122 = f32[64,128]{1,0:T(8,128)S(1)} all-gather(f32[8,128]{1,0:T(8,128)S(1)} %get-tuple-element.51), channel_id=1, replica_groups=mesh['sub'=8,'coarse'=4] {'sub'}, dimensions={0}, use_global_device_ids=true | all-gather | bytes 36864 | tf_op jit(solution)/shard_map/all_gather | solution.py:82
  393.3 9.0 all_gather.124
  402.3 8.3 all_gather.125
  413.5 37.6 %psum.96 = f32[2]{0:T(128)S(1)} all-reduce(f32[2]{0:T(128)S(1)} %pad_maximum_fusion.8), channel_id=1, replica_groups=mesh['sub'=8,'coarse'=4] {'sub','coarse'}, use_global_device_ids=true, to_apply=%region_12.14 | all-reduce | flops 2 | bytes 16 | tf_op jit(solution)/shard_map/psum | solution.py:125
  453.6 41.7 %psum.97 = f32[]{:T(128)} all-reduce(f32[]{:T(128)} %get-tuple-element.21), channel_id=1, replica_groups=mesh['sub'=8,'coarse'=4] {'sub','coarse'}, use_global_device_ids=true, to_apply=%region_14.16 | all-reduce | flops 1 | bytes 8 | tf_op jit(solution)/shard_map/psum | solution.py:94
  496.8 10.1 %all_gather.126 = f32[64,128]{1,0:T(8,128)S(1)} all-gather(f32[8,128]{1,0:T(8,128)S(1)} %get-tuple-element.47), channel_id=1, replica_groups=mesh['sub'=8,'coarse'=4] {'sub'}, dimensions={0}, use_global_device_ids=true | all-gather | bytes 36864 | tf_op jit(solution)/shard_map/all_gather | solution.py:82
  506.9 8.1 all_gather.127
  515.0 9.0 all_gather.128
  524.0 8.1 all_gather.129
  533.0 15.4 %fusion.2 = f32[128,1,128]{2,1,0:T(1,128)S(1)} fusion(f32[128,128,1]{1,2,0:T(1,128)S(1)} %bitcast.357, f32[1,1,128,128,128]{4,3,2,1,0:T(8,128)} %param.16), kind=kOutput, calls=%fused_computation.10 | convolution fusion | flops 25165824 | bytes 8519680 | tf_op jit(solution)/shard_map/bij,bj->bi/dot_general | solution.py:107
  548.6 37.7 %psum.98 = f32[512]{0:T(512)S(1)} all-reduce(f32[512]{0:T(512)S(1)} %broadcast_multiply_fusion.1), channel_id=1, replica_groups=mesh['sub'=8,'coarse'=4] {'sub','coarse'}, use_global_device_ids=true, to_apply=%region_16.18 | all-reduce | flops 512 | bytes 4096 | tf_op jit(solution)/shard_map/psum | solution.py:104
  586.5 9.6 %all-gather.2 = f32[4,1,128]{2,1,0:T(1,128)S(1)} all-gather(f32[1,1,128]{2,1,0:T(1,128)S(1)} %convolution_bitcast_fusion.3), channel_id=1, replica_groups=mesh['sub'=8,'coarse'=4] {'coarse'}, dimensions={0}, use_global_device_ids=true | all-gather | bytes 2560 | tf_op jit(solution)/shard_map/all_gather | solution.py:111
  597.2 9.8 %all_gather.131 = f32[64,128]{1,0:T(8,128)S(1)} all-gather(f32[8,128]{1,0:T(8,128)S(1)} %get-tuple-element.43), channel_id=1, replica_groups=mesh['sub'=8,'coarse'=4] {'sub'}, dimensions={0}, use_global_device_ids=true | all-gather | bytes 36864 | tf_op jit(solution)/shard_map/all_gather | solution.py:82
  607.0 9.0 all_gather.132
  616.1 8.5 all_gather.133
  624.6 9.0 all_gather.134
  637.2 37.6 %psum.99 = f32[3]{0:T(128)S(1)} all-reduce(f32[3]{0:T(128)S(1)} %pad_maximum_fusion.9), channel_id=1, replica_groups=mesh['sub'=8,'coarse'=4] {'sub','coarse'}, use_global_device_ids=true, to_apply=%region_20.22 | all-reduce | flops 3 | bytes 24 | tf_op jit(solution)/shard_map/psum | solution.py:125
  677.9 40.7 %psum.100 = f32[]{:T(128)} all-reduce(f32[]{:T(128)} %get-tuple-element.17), channel_id=1, replica_groups=mesh['sub'=8,'coarse'=4] {'sub','coarse'}, use_global_device_ids=true, to_apply=%region_22.24 | all-reduce | flops 1 | bytes 8 | tf_op jit(solution)/shard_map/psum | solution.py:94
  720.0 10.0 %all_gather.135 = f32[64,128]{1,0:T(8,128)S(1)} all-gather(f32[8,128]{1,0:T(8,128)S(1)} %get-tuple-element.39), channel_id=1, replica_groups=mesh['sub'=8,'coarse'=4] {'sub'}, dimensions={0}, use_global_device_ids=true | all-gather | bytes 36864 | tf_op jit(solution)/shard_map/all_gather | solution.py:82
  730.0 9.0 all_gather.136
  747.1 9.0 all_gather.138
  757.1 15.4 %fusion = f32[128,1,128]{2,1,0:T(1,128)S(1)} fusion(f32[128,128,1]{1,2,0:T(1,128)S(1)} %bitcast.358, f32[1,1,128,128,128]{4,3,2,1,0:T(8,128)} %param.16), kind=kOutput, calls=%fused_computation.8 | convolution fusion | flops 25165824 | bytes 8519680 | tf_op jit(solution)/shard_map/bij,bj->bi/dot_general | solution.py:107
  772.7 37.7 %psum.101 = f32[512]{0:T(512)S(1)} all-reduce(f32[512]{0:T(512)S(1)} %broadcast_multiply_fusion), channel_id=1, replica_groups=mesh['sub'=8,'coarse'=4] {'sub','coarse'}, use_global_device_ids=true, to_apply=%region_24.26 | all-reduce | flops 512 | bytes 4096 | tf_op jit(solution)/shard_map/psum | solution.py:104
  810.6 9.6 %all-gather.3 = f32[4,1,128]{2,1,0:T(1,128)S(1)} all-gather(f32[1,1,128]{2,1,0:T(1,128)S(1)} %convolution_bitcast_fusion.1), channel_id=1, replica_groups=mesh['sub'=8,'coarse'=4] {'coarse'}, dimensions={0}, use_global_device_ids=true | all-gather | bytes 2560 | tf_op jit(solution)/shard_map/all_gather | solution.py:111
  821.3 9.8 %all_gather.140 = f32[64,128]{1,0:T(8,128)S(1)} all-gather(f32[8,128]{1,0:T(8,128)S(1)} %get-tuple-element.35), channel_id=1, replica_groups=mesh['sub'=8,'coarse'=4] {'sub'}, dimensions={0}, use_global_device_ids=true | all-gather | bytes 36864 | tf_op jit(solution)/shard_map/all_gather | solution.py:82
  831.1 8.2 all_gather.141
  839.4 9.0 all_gather.142
  860.6 37.6 %psum.102 = f32[4]{0:T(128)S(1)} all-reduce(f32[4]{0:T(128)S(1)} %pad_maximum_fusion.10), channel_id=1, replica_groups=mesh['sub'=8,'coarse'=4] {'sub','coarse'}, use_global_device_ids=true, to_apply=%region_29.31 | all-reduce | flops 4 | bytes 32 | tf_op jit(solution)/shard_map/psum | solution.py:125
  908.5 41.8 %psum.103 = f32[]{:T(128)} all-reduce(f32[]{:T(128)} %multiply_reduce_fusion), channel_id=1, replica_groups=mesh['sub'=8,'coarse'=4] {'sub','coarse'}, use_global_device_ids=true, to_apply=%region_31.33 | all-reduce | flops 1 | bytes 8 | tf_op jit(solution)/shard_map/psum | solution.py:94
  (135 shorter events, 82.6 us)
Async XLA Ops:
  0.0 87.0 %copy-start = (f32[1,1,4,128,128]{4,3,2,1,0:T(8,128)S(1)}, f32[1,1,4,128,128]{4,3,2,1,0:T(8,128)}, u32[]{:S(2)}) copy-start(f32[1,1,4,128,128]{4,3,2,1,0:T(8,128)} %param.17) | copy-start | bytes 786436
  0.0 153.1 %copy-start.1 = (f32[1,1,128,128]{3,2,1,0:T(8,128)S(1)}, f32[1,1,128,128]{3,2,1,0:T(8,128)}, u32[]{:S(2)}) copy-start(f32[1,1,128,128]{3,2,1,0:T(8,128)} %param.18) | copy-start | bytes 196612
  0.0 103.2 %copy-start.5 = (s32[1,1,128]{2,1,0:T(1,128)S(1)}, s32[1,1,128]{2,1,0:T(1,128)}, u32[]{:S(2)}) copy-start(s32[1,1,128]{2,1,0:T(1,128)} %param.23) | copy-start | bytes 1540
  0.0 142.9 %copy-start.2 = (f32[128,512]{1,0:T(8,128)S(1)}, f32[128,512]{1,0:T(8,128)}, u32[]{:S(2)}) copy-start(f32[128,512]{1,0:T(8,128)} %param.19) | copy-start | bytes 786436
  0.0 190.4 %copy-start.3 = (f32[1,1,128,128]{3,2,1,0:T(8,128)S(1)}, f32[1,1,128,128]{3,2,1,0:T(8,128)}, u32[]{:S(2)}) copy-start(f32[1,1,128,128]{3,2,1,0:T(8,128)} %param.15) | copy-start | bytes 196612
  0.0 190.5 %copy-start.4 = (f32[1,1,128,128]{3,2,1,0:T(8,128)S(1)}, f32[1,1,128,128]{3,2,1,0:T(8,128)}, u32[]{:S(2)}) copy-start(f32[1,1,128,128]{3,2,1,0:T(8,128)} %param.14) | copy-start | bytes 196612
where the time goes:
time: 971 us; the launch traced here: 959 us
  blocking collectives  835 us (86%)
  matrix products  73.9 us (8%)
  other arithmetic  21.1 us (2%)
  between operations  20.1 us (2%)
    all_gather x32, blocking collectives, margin(): gathered = lax.all_gather(outgoing[round_id], 'sub', axis=0, tiled=True)  286 us
    psum x5, blocking collectives, squared_norm(): return lax.psum(jnp.sum(values * values), ('sub', 'coarse'))  208 us
    psum x4, blocking collectives, on_device(): lax.psum(jnp.dot(inner, member_table, precision=highest) * factor, ('sub'...  152 us
    psum x4, blocking collectives, on_device(): lax.psum(jnp.stack([jnp.sum(vector * product) for vector in basis_list]),...  151 us
    dot_general x4, matrix products, on_device(): jnp.einsum('bij,bj->bi', inverse_blocks, current + margin(current), preci...  61.5 us
    all_gather x4, blocking collectives, on_device(): coarse_full = lax.all_gather(coarse_part, 'coarse', axis=0, tiled=True)  38.7 us

commit v1 on v0

--- a/solution.py
+++ b/solution.py
@@ -108,7 +108,16 @@
             "bij,bj->bi", inverse_blocks, current + margin(current), precision=highest
         )
         coarse_part = jnp.dot(coarse_inverse, restricted, precision=highest)
-        coarse_full = lax.all_gather(coarse_part, "coarse", axis=0, tiled=True)
+        ring = [coarse_part]
+        for hop in range(3):
+            ring.append(
+                lax.ppermute(ring[-1], "coarse", [(dev, (dev + 1) % 4) for dev in range(4)])
+            )
+        coarse_full = jnp.roll(
+            jnp.concatenate(ring[::-1], axis=0),
+            (lax.axis_index("coarse") + 1) * ring[0].shape[0],
+            axis=0,
+        )
         prolonged = jnp.dot(member_table, coarse_full, precision=highest)
         direction = local_part + prolonged[:, None] * basis_local
         directions.append(direction)

time: 971 us -> 937 us (0.965)
  matrix products: 73.9 us -> 13.6 us
  blocking collectives: 835 us -> 797 us
  waiting for transfers between devices: 0 us -> 25 us
  other arithmetic: 21.1 us -> 42.5 us
  starting transfers between devices: 0 us -> 11.7 us
    dot_general x4 -> x0, matrix products: 61.5 us -> none  [on_device(): jnp.einsum('bij,bj->bi', inverse_blocks, current + margin(current), preci...]
    all_gather x4 -> x0, blocking collectives: 38.7 us -> none  [on_device(): coarse_full = lax.all_gather(coarse_part, 'coarse', axis=0, tiled=True)]
    ppermute x0 -> x12, waiting for transfers between devices: none -> 25 us  [on_device(): lax.ppermute(ring[-1], 'coarse', [(dev, (dev + 1) % 4) for dev in range(4)])]
    unnamed x0 -> x4, other arithmetic: none -> 22.5 us
    ppermute x0 -> x12, starting transfers between devices: none -> 11.7 us  [on_device(): lax.ppermute(ring[-1], 'coarse', [(dev, (dev + 1) % 4) for dev in range(4)])]
  transfers between devices with their start and end apart: 0 -> 12, of which waited for: 0 -> 6; matrix products, arithmetic and copies ran while one was open for 0% -> 4% of each run, Pallas kernels for 0% -> 0%
where the time goes in v1:
time: 937 us; the launch traced here: 925 us
  blocking collectives  797 us (85%)
  other arithmetic  42.5 us (5%)
  waiting for transfers between devices  25 us (3%)
  between operations  21.1 us (2%)
  local copies, waits for them, and re-layouts  14.2 us (2%)
  matrix products  13.6 us (1%)
  starting transfers between devices  11.7 us (1%)
    all_gather x32, blocking collectives, margin(): gathered = lax.all_gather(outgoing[round_id], 'sub', axis=0, tiled=True)  279 us
    psum x5, blocking collectives, squared_norm(): return lax.psum(jnp.sum(values * values), ('sub', 'coarse'))  210 us
    psum x4, blocking collectives, on_device(): lax.psum(jnp.dot(inner, member_table, precision=highest) * factor, ('sub'...  158 us
    psum x4, blocking collectives, on_device(): lax.psum(jnp.stack([jnp.sum(vector * product) for vector in basis_list]),...  150 us
    ppermute x12, waiting for transfers between devices, on_device(): lax.ppermute(ring[-1], 'coarse', [(dev, (dev + 1) % 4) for dev in range(4)])  25 us
    unnamed x4, other arithmetic  22.5 us
  transfers between devices with their start and end apart: 12, of which 6 were waited for; matrix products, arithmetic and copies ran while one was open for 4% of the time, Pallas kernels for 0%

profile of v1, /device:TPU:0, one launch (start us, length us, event | category | flops | bytes accessed | tf_op | source)
XLA Modules:
  0.0 925.2 jit_solution(2926567250989327984)
XLA Ops:
  2.5 42.3 %psum.91 = f32[]{:T(128)} all-reduce(f32[]{:T(128)} %multiply_reduce_fusion.14), channel_id=1, replica_groups=mesh['sub'=8,'coarse'=4] {'sub','coarse'}, use_global_device_ids=true, to_apply=%region_1.0 | all-reduce | flops 1 | bytes 8 | tf_op jit(solution)/shard_map/psum | solution.py:94
  47.3 40.3 %psum.92 = f32[512]{0:T(512)S(1)} all-reduce(f32[512]{0:T(512)S(1)} %broadcast_multiply_fusion.3), channel_id=1, replica_groups=mesh['sub'=8,'coarse'=4] {'sub','coarse'}, use_global_device_ids=true, to_apply=%region_3.5 | all-reduce | flops 512 | bytes 4096 | tf_op jit(solution)/shard_map/psum | solution.py:104
  95.8 9.8 %all_gather.96 = f32[64,128]{1,0:T(8,128)S(1)} all-gather(f32[8,128]{1,0:T(8,128)S(1)} %get-tuple-element.64), channel_id=1, replica_groups=mesh['sub'=8,'coarse'=4] {'sub'}, dimensions={0}, use_global_device_ids=true | all-gather | bytes 36864 | tf_op jit(solution)/shard_map/all_gather | solution.py:82
  105.6 9.0 all_gather.99
  114.6 8.1 all_gather.98
  122.7 9.0 all_gather.97
  132.6 5.6 fusion
  150.2 8.1 all_gather.100
  158.3 9.0 all_gather.103
  167.3 8.1 all_gather.102
  175.4 9.0 all_gather.101
  186.2 37.1 %psum.93 = f32[]{:T(128)} all-reduce(f32[]{:T(128)} %get-tuple-element.81), channel_id=1, replica_groups=mesh['sub'=8,'coarse'=4] {'sub','coarse'}, use_global_device_ids=true, to_apply=%region_5.8 | all-reduce | flops 1 | bytes 8 | tf_op jit(solution)/shard_map/psum | solution.py:134
  224.6 41.8 %psum.94 = f32[]{:T(128)} all-reduce(f32[]{:T(128)} %multiply_reduce_fusion.12), channel_id=1, replica_groups=mesh['sub'=8,'coarse'=4] {'sub','coarse'}, use_global_device_ids=true, to_apply=%region_7.10 | all-reduce | flops 1 | bytes 8 | tf_op jit(solution)/shard_map/psum | solution.py:94
  268.1 39.6 %psum.95 = f32[512]{0:T(512)S(1)} all-reduce(f32[512]{0:T(512)S(1)} %broadcast_multiply_fusion.2), channel_id=1, replica_groups=mesh['sub'=8,'coarse'=4] {'sub','coarse'}, use_global_device_ids=true, to_apply=%region_9.12 | all-reduce | flops 512 | bytes 4096 | tf_op jit(solution)/shard_map/psum | solution.py:104
  311.3 9.8 %all_gather.104 = f32[64,128]{1,0:T(8,128)S(1)} all-gather(f32[8,128]{1,0:T(8,128)S(1)} %get-tuple-element.56), channel_id=1, replica_groups=mesh['sub'=8,'coarse'=4] {'sub'}, dimensions={0}, use_global_device_ids=true | all-gather | bytes 36864 | tf_op jit(solution)/shard_map/all_gather | solution.py:82
  321.1 8.1 all_gather.107
  329.3 9.0 all_gather.106
  338.3 8.1 all_gather.105
  352.3 5.6 fusion.1
  361.2 9.0 all_gather.108
  370.2 8.1 all_gather.111
  378.4 9.0 all_gather.110
  387.3 8.1 all_gather.109
  398.8 39.1 %psum.96 = f32[2]{0:T(128)S(1)} all-reduce(f32[2]{0:T(128)S(1)} %pad_maximum_fusion.8), channel_id=1, replica_groups=mesh['sub'=8,'coarse'=4] {'sub','coarse'}, use_global_device_ids=true, to_apply=%region_12.15 | all-reduce | flops 2 | bytes 16 | tf_op jit(solution)/shard_map/psum | solution.py:134
  440.6 41.7 %psum.97 = f32[]{:T(128)} all-reduce(f32[]{:T(128)} %get-tuple-element.22), channel_id=1, replica_groups=mesh['sub'=8,'coarse'=4] {'sub','coarse'}, use_global_device_ids=true, to_apply=%region_14.17 | all-reduce | flops 1 | bytes 8 | tf_op jit(solution)/shard_map/psum | solution.py:94
  483.2 38.7 %psum.98 = f32[512]{0:T(512)S(1)} all-reduce(f32[512]{0:T(512)S(1)} %broadcast_multiply_fusion.1), channel_id=1, replica_groups=mesh['sub'=8,'coarse'=4] {'sub','coarse'}, use_global_device_ids=true, to_apply=%region_16.19 | all-reduce | flops 512 | bytes 4096 | tf_op jit(solution)/shard_map/psum | solution.py:104
  525.1 9.8 %all_gather.112 = f32[64,128]{1,0:T(8,128)S(1)} all-gather(f32[8,128]{1,0:T(8,128)S(1)} %get-tuple-element.48), channel_id=1, replica_groups=mesh['sub'=8,'coarse'=4] {'sub'}, dimensions={0}, use_global_device_ids=true | all-gather | bytes 36864 | tf_op jit(solution)/shard_map/all_gather | solution.py:82
  534.9 9.0 all_gather.115
  543.9 8.1 all_gather.114
  552.0 9.1 all_gather.113
  578.4 8.1 all_gather.116
  586.5 9.0 all_gather.119
  595.5 8.1 all_gather.118
  603.6 9.0 all_gather.117
  616.5 36.8 %psum.99 = f32[3]{0:T(128)S(1)} all-reduce(f32[3]{0:T(128)S(1)} %pad_maximum_fusion.9), channel_id=1, replica_groups=mesh['sub'=8,'coarse'=4] {'sub','coarse'}, use_global_device_ids=true, to_apply=%region_20.23 | all-reduce | flops 3 | bytes 24 | tf_op jit(solution)/shard_map/psum | solution.py:134
  656.6 41.6 %psum.100 = f32[]{:T(128)} all-reduce(f32[]{:T(128)} %get-tuple-element.18), channel_id=1, replica_groups=mesh['sub'=8,'coarse'=4] {'sub','coarse'}, use_global_device_ids=true, to_apply=%region_22.25 | all-reduce | flops 1 | bytes 8 | tf_op jit(solution)/shard_map/psum | solution.py:94
  699.1 39.6 %psum.101 = f32[512]{0:T(512)S(1)} all-reduce(f32[512]{0:T(512)S(1)} %broadcast_multiply_fusion), channel_id=1, replica_groups=mesh['sub'=8,'coarse'=4] {'sub','coarse'}, use_global_device_ids=true, to_apply=%region_24.27 | all-reduce | flops 512 | bytes 4096 | tf_op jit(solution)/shard_map/psum | solution.py:104
  741.9 9.8 %all_gather.120 = f32[64,128]{1,0:T(8,128)S(1)} all-gather(f32[8,128]{1,0:T(8,128)S(1)} %get-tuple-element.40), channel_id=1, replica_groups=mesh['sub'=8,'coarse'=4] {'sub'}, dimensions={0}, use_global_device_ids=true | all-gather | bytes 36864 | tf_op jit(solution)/shard_map/all_gather | solution.py:82
  751.7 8.1 all_gather.123
  759.9 9.0 all_gather.122
  768.9 8.3 all_gather.121
  778.1 5.6 fusion.3
  796.2 9.0 all_gather.124
  805.2 8.1 all_gather.127
  813.3 9.0 all_gather.126
  822.3 8.1 all_gather.125
  835.0 36.8 %psum.102 = f32[4]{0:T(128)S(1)} all-reduce(f32[4]{0:T(128)S(1)} %pad_maximum_fusion.10), channel_id=1, replica_groups=mesh['sub'=8,'coarse'=4] {'sub','coarse'}, use_global_device_ids=true, to_apply=%region_29.32 | all-reduce | flops 4 | bytes 32 | tf_op jit(solution)/shard_map/psum | solution.py:134
  880.8 42.5 %psum.103 = f32[]{:T(128)} all-reduce(f32[]{:T(128)} %multiply_reduce_fusion), channel_id=1, replica_groups=mesh['sub'=8,'coarse'=4] {'sub','coarse'}, use_global_device_ids=true, to_apply=%region_31.34 | all-reduce | flops 1 | bytes 8 | tf_op jit(solution)/shard_map/psum | solution.py:94
  (197 shorter events, 90.2 us)
Async XLA Ops:
  0.0 131.7 %copy-start = (f32[1,1,4,128,128]{4,3,2,1,0:T(8,128)S(1)}, f32[1,1,4,128,128]{4,3,2,1,0:T(8,128)}, u32[]{:S(2)}) copy-start(f32[1,1,4,128,128]{4,3,2,1,0:T(8,128)} %param.19) | copy-start | bytes 786436
  0.0 149.1 %copy-start.4 = (s32[1,1,128]{2,1,0:T(1,128)S(1)}, s32[1,1,128]{2,1,0:T(1,128)}, u32[]{:S(2)}) copy-start(s32[1,1,128]{2,1,0:T(1,128)} %param.25) | copy-start | bytes 1540
  0.0 307.7 %copy-start.1 = (f32[128,512]{1,0:T(8,128)S(1)}, f32[128,512]{1,0:T(8,128)}, u32[]{:S(2)}) copy-start(f32[128,512]{1,0:T(8,128)} %param.21) | copy-start | bytes 786436
  0.0 143.7 %copy-start.3 = (f32[1,1,128,128]{3,2,1,0:T(8,128)S(1)}, f32[1,1,128,128]{3,2,1,0:T(8,128)}, u32[]{:S(2)}) copy-start(f32[1,1,128,128]{3,2,1,0:T(8,128)} %param.16) | copy-start | bytes 196612
  0.0 143.8 %copy-start.2 = (f32[1,1,128,128]{3,2,1,0:T(8,128)S(1)}, f32[1,1,128,128]{3,2,1,0:T(8,128)}, u32[]{:S(2)}) copy-start(f32[1,1,128,128]{3,2,1,0:T(8,128)} %param.17) | copy-start | bytes 196612
  88.9 49.4 %collective-permute-start = (f32[128]{0:T(128)S(1)}, f32[128]{0:T(128)S(1)}, u32[]{:S(2)}, u32[]{:S(2)}) collective-permute-start(f32[128]{0:T(128)S(1)} %convolution_bitcast_fusion.7), channel_id=1, source_target_pairs={{0,1},{1,2},{2,3},{3,0},{4,5},{5,6},{6,7},{7,4},{8,9},{9,10},{10,1... | collective-permute-start | bytes 1544 | tf_op jit(solution)/shard_map/ppermute | solution.py:114
  138.3 5.4 collective-permute-start.1
  143.7 5.3 collective-permute-start.2
  308.0 38.9 %collective-permute-start.3 = (f32[128]{0:T(128)S(1)}, f32[128]{0:T(128)S(1)}, u32[]{:S(2)}, u32[]{:S(2)}) collective-permute-start(f32[128]{0:T(128)S(1)} %convolution_bitcast_fusion.5), channel_id=1, source_target_pairs={{0,1},{1,2},{2,3},{3,0},{4,5},{5,6},{6,7},{7,4},{8,9},{9,10},{10,1... | collective-permute-start | bytes 1544 | tf_op jit(solution)/shard_map/ppermute | solution.py:114
  346.9 5.4 collective-permute-start.4
  352.3 7.8 collective-permute-start.5
  522.2 39.9 %collective-permute-start.6 = (f32[128]{0:T(128)S(1)}, f32[128]{0:T(128)S(1)}, u32[]{:S(2)}, u32[]{:S(2)}) collective-permute-start(f32[128]{0:T(128)S(1)} %convolution_bitcast_fusion.3), channel_id=1, source_target_pairs={{0,1},{1,2},{2,3},{3,0},{4,5},{5,6},{6,7},{7,4},{8,9},{9,10},{10,1... | collective-permute-start | bytes 1544 | tf_op jit(solution)/shard_map/ppermute | solution.py:114
  562.1 9.7 %collective-permute-start.7 = (f32[128]{0:T(128)S(1)}, f32[128]{0:T(128)S(1)}, u32[]{:S(2)}, u32[]{:S(2)}) collective-permute-start(f32[128]{0:T(128)S(1)} %collective-permute-done.6), channel_id=1, source_target_pairs={{0,1},{1,2},{2,3},{3,0},{4,5},{5,6},{6,7},{7,4},{8,9},{9,10},{10,1... | collective-permute-start | bytes 1544 | tf_op jit(solution)/shard_map/ppermute | solution.py:114
  571.8 5.4 collective-permute-start.8
  739.0 45.3 %collective-permute-start.9 = (f32[128]{0:T(128)S(1)}, f32[128]{0:T(128)S(1)}, u32[]{:S(2)}, u32[]{:S(2)}) collective-permute-start(f32[128]{0:T(128)S(1)} %convolution_bitcast_fusion.1), channel_id=1, source_target_pairs={{0,1},{1,2},{2,3},{3,0},{4,5},{5,6},{6,7},{7,4},{8,9},{9,10},{10,1... | collective-permute-start | bytes 1544 | tf_op jit(solution)/shard_map/ppermute | solution.py:114
  784.3 5.4 collective-permute-start.10
  789.7 5.3 collective-permute-start.11
